TPU v7x, 128 devices: a whole 4x4x4 slice. The times are simulated.
128 devices in a mesh: row: 16 (over x, y), col: 8 (over z, core).
Axes of the slice: x: 4, y: 4, z: 4, core: 2. Of those that a mesh axis runs over, the one named last changes fastest.
Arguments:
- raw_rows: bfloat16 [131072, 64], P(('row', 'col')), may hold values from -6 to 6
- raw_wide: int32 [131072], P(('row', 'col')), may hold values from 0 to 1
- raw_dest: int32 [131072], P(('row', 'col')), may hold values from 0 to 127, as said below
- raw_slot: int32 [131072], P(('row', 'col')), may hold values from 0 to 511
- proj_narrow: bfloat16 [32, 128], replicated, may hold values from -1 to 1
- proj_wide: bfloat16 [64, 128], replicated, may hold values from -0.75 to 0.75
- adj_values: bfloat16 [32768, 32768], P('row', 'col'), may hold values from -1 to 1
- tile_mask: int32 [256, 256], P('row', 'col'), may hold values 0 or 1
- tile_scale: float32 [256, 256], P('row', 'col'), may hold values from 0.0041432036 to 0.041432038
- weight_sum: bfloat16 [2, 128, 128], replicated, may hold values from -0.5 to 0.5
- weight_product: bfloat16 [2, 128, 128], replicated, may hold values from -0.5 to 0.5
Outputs:
- user_out: bfloat16 [32768, 128], P(('row', 'col'))
- item_out: bfloat16 [8, 4096, 128], P('col', 'row')
Inputs may be any that keep to these rules, and one draw needn't show every extreme that they name: `raw_dest`: among the feature rows stored on one device at most 24 have any one destination; one device, drawn from the seed, is the destination of exactly 24 rows of every device.
All inputs are finite; a program needn't handle non-finite values. No bound on the sum of `tile_mask` on one device may be relied on, other than what follows from the above.
Results may differ from a plain program's by a relative error of at most 0.025.
Values may be sent and summed in bfloat16 or wider, within the bound.
A program may use at most 128 MiB of HBM per device.

v0:
```python
import jax
import jax.numpy as jnp
from jax import lax
from jax.sharding import PartitionSpec as P

D = 128
RAW_COLS = 64
NARROW = 32
TILE = 128
LAYERS = 2
UPD = 256
IPD = 256


def dequantize(values_bf, mask_tiles, scale_tiles):
    row_count = values_bf.shape[0]
    columns = values_bf.shape[1]
    values = values_bf.astype(jnp.float32)
    factor = mask_tiles.astype(jnp.float32) * scale_tiles
    tiled = (
        values.reshape(row_count // TILE, TILE, columns // TILE, TILE) * factor[:, None, :, None]
    )
    return tiled.reshape(row_count, columns).astype(jnp.bfloat16)


def update(side_sum, own_rows, weight_sum, weight_product):
    own_float = own_rows.astype(jnp.float32)
    summed = (side_sum + own_float).astype(jnp.bfloat16)
    product = (side_sum * own_float).astype(jnp.bfloat16)
    linear = jnp.dot(summed, weight_sum, preferred_element_type=jnp.float32)
    linear = linear + jnp.dot(product, weight_product, preferred_element_type=jnp.float32)
    return jnp.where(linear > 0, linear, 0.2 * linear).astype(jnp.bfloat16)


def per_device(
    raw_rows,
    raw_wide,
    raw_dest,
    raw_slot,
    proj_narrow,
    proj_wide,
    adj_values,
    tile_mask,
    tile_scale,
    weight_sum,
    weight_product,
):
    row_size = lax.axis_size("row")
    col_size = lax.axis_size("col")
    devices = row_size * col_size
    capacity = 3 * raw_rows.shape[0] // devices
    node_count = UPD + IPD
    targets = jnp.arange(devices, dtype=jnp.int32)
    onehot = (raw_dest[:, None] == targets[None, :]).astype(jnp.int32)
    rank_in_pair = jnp.sum((jnp.cumsum(onehot, axis=0) - onehot) * onehot, axis=1)
    position = raw_dest * capacity + rank_in_pair
    send_rows = jnp.zeros((devices * capacity, RAW_COLS), jnp.bfloat16).at[position].set(raw_rows)
    send_rows = send_rows.reshape(devices, capacity, RAW_COLS)
    send_codes = (
        jnp.full((devices * capacity,), -1, jnp.int32).at[position].set(raw_slot * 2 + raw_wide)
    )
    send_codes = send_codes.reshape(devices, capacity)
    rows_in = lax.all_to_all(send_rows, ("row", "col"), split_axis=0, concat_axis=0, tiled=True)
    codes_in = lax.all_to_all(send_codes, ("row", "col"), split_axis=0, concat_axis=0, tiled=True)
    wide_part = jnp.einsum("psc,cd->psd", rows_in, proj_wide, preferred_element_type=jnp.float32)
    narrow_part = jnp.einsum(
        "psc,cd->psd", rows_in[:, :, :NARROW], proj_narrow, preferred_element_type=jnp.float32
    )
    chosen = jnp.where((codes_in % 2 == 1)[:, :, None], wide_part, narrow_part)
    flat_codes = codes_in.reshape(-1)
    segment = jnp.where(flat_codes >= 0, flat_codes // 2, node_count).astype(jnp.int32)
    initial = jax.ops.segment_sum(chosen.reshape(-1, D), segment, num_segments=node_count + 1)
    initial = initial[:node_count].astype(jnp.bfloat16)
    user_rows = initial[:UPD]
    item_rows = initial[UPD:]
    adjacency = dequantize(adj_values, tile_mask, tile_scale)
    for layer_index in range(LAYERS):
        user_part = jnp.dot(
            adjacency,
            lax.all_gather(item_rows, "row", axis=0, tiled=True),
            preferred_element_type=jnp.float32,
        )
        item_part = lax.dot_general(
            adjacency,
            lax.all_gather(user_rows, "col", axis=0, tiled=True),
            (((0,), (0,)), ((), ())),
            preferred_element_type=jnp.float32,
        )
        user_side = lax.psum_scatter(
            user_part.astype(jnp.bfloat16), "col", scatter_dimension=0, tiled=True
        ).astype(jnp.float32)
        item_side = lax.psum_scatter(
            item_part.astype(jnp.bfloat16), "row", scatter_dimension=0, tiled=True
        ).astype(jnp.float32)
        new_users = update(
            user_side, user_rows, weight_sum[layer_index], weight_product[layer_index]
        )
        new_items = update(
            item_side, item_rows, weight_sum[layer_index], weight_product[layer_index]
        )
        user_rows = new_users
        item_rows = new_items
    return (user_rows, item_rows[None])


def solution(mesh):
    placed = (
        P(("row", "col"), None),
        P(("row", "col")),
        P(("row", "col")),
        P(("row", "col")),
        P(),
        P(),
        P("row", "col"),
        P("row", "col"),
        P("row", "col"),
        P(),
        P(),
    )
    return jax.shard_map(
        per_device,
        mesh=mesh,
        in_specs=placed,
        out_specs=(P(("row", "col"), None), P("col", "row", None)),
        check_vma=False,
    )
```

profile of v0, /device:TPU:1, one launch (start us, length us, event | category | flops | bytes accessed | tf_op | source)
XLA Modules:
  0.0 391.2 jit_solution(6186443028379261932)
XLA Ops:
  7.2 0.0 copy-start
  7.2 0.8 copy.19
  8.0 0.2 fusion.3
  8.3 0.1 copy.20
  8.4 1.0 fusion.2
  9.4 0.7 compare_select_fusion.8
  10.2 4.3 %scatter_custom_fusion = s32[3072]{0:T(1024)S(1)} fusion(s32[1024]{0:T(1024)S(1)} %get-tuple-element.4, s32[1024]{0:T(1024)S(1)} %get-tuple-element.5, s32[]{:T(128)} %constant.40.clone.1), kind=kCustom, calls=%fused_computation.88 | custom fusion | bytes 12292 | tf_op jit(solution)/shard_map/scatter | solution.py:60
  14.5 0.7 all_to_all.11
  15.2 11.5 %all-to-all-start = ((s32[128,1,24]{2,1,0:T(1,128)}), s32[128,1,24]{2,1,0:T(1,128)S(1)}, u32[]{:S(2)}, u32[]{:S(2)}) async-start(s32[128,1,24]{2,1,0:T(1,128)} %bitcast.4), calls=%async_computation | async-start | bytes 131072 | tf_op jit(solution)/shard_map/all_to_all | solution.py:64
  26.7 0.7 convert_multiply_fusion.4
  27.4 1.1 copy.23
  28.5 3.4 scatter_custom_fusion.1
  32.0 1.2 reshape.189
  33.2 2.8 all-to-all-done
  36.0 6.9 %all-to-all-start.1 = ((bf16[128,2,768]{2,1,0:T(2,128)(2,1)}), bf16[128,2,768]{2,1,0:T(2,128)(2,1)S(1)}, u32[]{:S(2)}, u32[]{:S(2)}) async-start(bf16[128,2,768]{2,1,0:T(2,128)(2,1)} %reshape.189), calls=%async_computation.1 | async-start | bytes 786432 | tf_op jit(solution)/shard_map/all_to_all | solution.py:63
  42.9 0.0 all-gather.5.cloned.1.call-start
  43.0 0.5 broadcast.147
  43.5 0.8 reduce.3
  44.3 0.1 reshape.143
  44.5 0.1 copy.22
  44.5 0.1 compare_select_fusion.4
  44.6 10.6 %all-to-all-done.1 = bf16[128,2,768]{2,1,0:T(2,128)(2,1)S(1)} async-done(((bf16[128,2,768]{2,1,0:T(2,128)(2,1)}), bf16[128,2,768]{2,1,0:T(2,128)(2,1)S(1)}, u32[]{:S(2)}, u32[]{:S(2)}) %all-to-all-start.1) | async-done | bytes 393248 | tf_op jit(solution)/shard_map/all_to_all | solution.py:63
  55.2 0.5 reshape.190
  55.7 0.5 copy.24
  56.2 0.0 copy-done
  56.2 0.4 fusion.54
  56.6 1.4 convolution_select_fusion
  58.0 0.9 copy.26
  58.9 17.3 %scatter_custom_fusion.2 = f32[513,128]{1,0:T(8,128)S(1)} fusion(s32[3072]{0:T(1024)S(1)} %bitcast.64, f32[3072,128]{1,0:T(8,128)S(1)} %bitcast.61, f32[]{:T(128)} %constant.23.clone.1), kind=kCustom, calls=%fused_computation.43 | custom fusion | flops 393216 | bytes 262660 | tf_op jit(solution)/shard_map/scatter-add | solution.py:72
  76.3 0.6 fusion.63
  76.9 0.0 all-gather.5.cloned.1.call-update
  76.9 0.2 reduce-scatter.5.cloned.1.call-start
  77.2 4.9 %mul.54 = f32[16,128,32,128]{3,2,1,0:T(8,128)S(1)} broadcast(f32[16,32]{1,0:T(8,128)S(1)} %convert_multiply_fusion.4), dimensions={0,2} | broadcast | bytes 33556480 | tf_op jit(solution)/shard_map/mul | solution.py:21
  82.1 26.4 %fusion = bf16[2048,4096]{1,0:T(8,128)(2,1)} fusion(f32[256,8,32,128]{3,2,1,0:T(8,128)S(1)} %bitcast.59, bf16[2048,4096]{1,0:T(8,128)(2,1)} %param.17), kind=kLoop, calls=%fused_computation.4 | loop fusion | flops 25165824 | bytes 67108864 | tf_op jit(solution)/shard_map/convert_element_type | solution.py:23
  108.5 14.1 %all_gather.12 = bf16[2048,128]{1,0:T(8,128)(2,1)S(1)} all-gather(bf16[256,128]{1,0:T(8,128)(2,1)S(1)} %get-tuple-element.2), channel_id=1, replica_groups=mesh['row'=16,'col'=8] {'col'}, dimensions={0}, use_global_device_ids=true | all-gather | bytes 589824 | tf_op jit(solution)/shard_map/all_gather | solution.py:85
  122.6 9.3 %convolution_convert_fusion.1 = bf16[4096,128]{1,0:T(8,128)(2,1)} fusion(bf16[2048,4096]{1,0:T(8,128)(2,1)} %fusion, bf16[2048,128]{1,0:T(8,128)(2,1)S(1)} %all_gather.12), kind=kOutput, calls=%fused_computation.6 | convolution fusion | flops 2148007936 | bytes 18350080 | tf_op jit(solution)/shard_map/dot_general | solution.py:83
  131.9 0.0 reduce-scatter.5.cloned.1.call-update
  131.9 0.0 reduce-scatter.9.cloned.1.call-start
  131.9 0.0 all-gather.5.cloned.1.call-done
  132.0 11.4 %convolution_convert_fusion.2 = bf16[2048,128]{1,0:T(8,128)(2,1)} fusion(bf16[2048,4096]{1,0:T(8,128)(2,1)} %fusion, bf16[4096,128]{1,0:T(8,128)(2,1)} %all-gather.5.cloned.1.call-done), kind=kOutput, calls=%fused_computation.7 | convolution fusion | flops 2147745792 | bytes 18350080 | tf_op jit(solution)/shard_map/dot_general | solution.py:78
  143.3 0.0 reduce-scatter.9.cloned.1.call-update
  143.4 0.0 all-gather.3.cloned.1.call-start
  143.4 54.8 %reduce-scatter.5.cloned.1.call-done = bf16[256,128]{1,0:T(8,128)(2,1)} async-done(((bf16[4096,128]{1,0:T(8,128)(2,1)}), bf16[256,128]{1,0:T(8,128)(2,1)}) %reduce-scatter.5.cloned.1.call-update) | async-done | bytes 65552 | tf_op jit(solution)/shard_map/reduce_scatter | solution.py:92
  198.2 0.0 copy-done.3
  198.2 1.0 fusion.36
  199.2 1.6 fusion.13
  200.9 0.0 all-gather.3.cloned.1.call-update
  200.9 0.0 reduce-scatter.11.cloned.1.call-start
  200.9 29.0 %reduce-scatter.9.cloned.1.call-done = bf16[256,128]{1,0:T(8,128)(2,1)} async-done(((bf16[2048,128]{1,0:T(8,128)(2,1)}), bf16[256,128]{1,0:T(8,128)(2,1)}) %reduce-scatter.9.cloned.1.call-update) | async-done | bytes 65552 | tf_op jit(solution)/shard_map/reduce_scatter | solution.py:89
  230.0 1.0 fusion.33
  230.9 1.0 fusion.12
  232.0 16.7 %all_gather.15 = bf16[2048,128]{1,0:T(8,128)(2,1)S(1)} all-gather(bf16[256,128]{1,0:T(8,128)(2,1)S(1)} %fusion.12), channel_id=1, replica_groups=mesh['row'=16,'col'=8] {'col'}, dimensions={0}, use_global_device_ids=true | all-gather | bytes 589824 | tf_op jit(solution)/shard_map/all_gather | solution.py:85
  248.7 9.3 %convolution_convert_fusion = bf16[4096,128]{1,0:T(8,128)(2,1)} fusion(bf16[2048,4096]{1,0:T(8,128)(2,1)} %fusion, bf16[2048,128]{1,0:T(8,128)(2,1)S(1)} %all_gather.15), kind=kOutput, calls=%fused_computation.5 | convolution fusion | flops 2148007936 | bytes 18350080 | tf_op jit(solution)/shard_map/dot_general | solution.py:83
  258.0 0.0 reduce-scatter.11.cloned.1.call-update
  258.0 0.0 reduce-scatter.7.cloned.1.call-start
  258.1 17.3 %all-gather.3.cloned.1.call-done = bf16[4096,128]{1,0:T(8,128)(2,1)} async-done(((bf16[256,128]{1,0:T(8,128)(2,1)}), bf16[4096,128]{1,0:T(8,128)(2,1)}) %all-gather.3.cloned.1.call-update) | async-done | bytes 1048592 | tf_op jit(solution)/shard_map/all_gather | solution.py:80
  275.3 11.3 %convolution_convert_fusion.3 = bf16[2048,128]{1,0:T(8,128)(2,1)} fusion(bf16[2048,4096]{1,0:T(8,128)(2,1)} %fusion, bf16[4096,128]{1,0:T(8,128)(2,1)} %all-gather.3.cloned.1.call-done), kind=kOutput, calls=%fused_computation.8 | convolution fusion | flops 2147745792 | bytes 18350080 | tf_op jit(solution)/shard_map/dot_general | solution.py:78
  286.7 0.0 reduce-scatter.7.cloned.1.call-update
  286.7 63.5 %reduce-scatter.11.cloned.1.call-done = bf16[256,128]{1,0:T(8,128)(2,1)} async-done(((bf16[4096,128]{1,0:T(8,128)(2,1)}), bf16[256,128]{1,0:T(8,128)(2,1)}) %reduce-scatter.11.cloned.1.call-update) | async-done | bytes 65552 | tf_op jit(solution)/shard_map/reduce_scatter | solution.py:92
  350.2 1.0 fusion.27
  351.2 1.6 fusion.10
  352.8 28.9 %reduce-scatter.7.cloned.1.call-done = bf16[256,128]{1,0:T(8,128)(2,1)} async-done(((bf16[2048,128]{1,0:T(8,128)(2,1)}), bf16[256,128]{1,0:T(8,128)(2,1)}) %reduce-scatter.7.cloned.1.call-update) | async-done | bytes 65552 | tf_op jit(solution)/shard_map/reduce_scatter | solution.py:89
  381.8 1.0 fusion.30
  382.7 1.6 fusion.11
  (13 shorter events, 0.1 us)
Async XLA Ops:
  7.2 49.0 %copy-start = (bf16[64,128]{1,0:T(8,128)(2,1)S(1)}, bf16[64,128]{1,0:T(8,128)(2,1)}, u32[]{:S(2)}) copy-start(bf16[64,128]{1,0:T(8,128)(2,1)} %param.16) | copy-start | bytes 49156
  15.2 20.8 %all-to-all-start = ((s32[128,1,24]{2,1,0:T(1,128)}), s32[128,1,24]{2,1,0:T(1,128)S(1)}, u32[]{:S(2)}, u32[]{:S(2)}) async-start(s32[128,1,24]{2,1,0:T(1,128)} %bitcast.4), calls=%async_computation | async-start | bytes 131072 | tf_op jit(solution)/shard_map/all_to_all | solution.py:64
  36.0 19.2 %all-to-all-start.1 = ((bf16[128,2,768]{2,1,0:T(2,128)(2,1)}), bf16[128,2,768]{2,1,0:T(2,128)(2,1)S(1)}, u32[]{:S(2)}, u32[]{:S(2)}) async-start(bf16[128,2,768]{2,1,0:T(2,128)(2,1)} %reshape.189), calls=%async_computation.1 | async-start | bytes 786432 | tf_op jit(solution)/shard_map/all_to_all | solution.py:63
  42.9 89.0 %all-gather.5.cloned.1.call-start = ((), (), s32[]{:S(2)}) async-start(), calls=%async_computation.9 | async-start | bytes 1114112 | tf_op jit(solution)/shard_map/all_gather | solution.py:80
  76.9 121.3 %reduce-scatter.5.cloned.1.call-start = ((), (), s32[]{:S(2)}) async-start(), calls=%async_computation.6 | async-start | bytes 1114112 | tf_op jit(solution)/shard_map/reduce_scatter | solution.py:92
  131.9 66.4 %copy-start.3 = (bf16[2,128,128]{2,1,0:T(8,128)(2,1)S(1)}, bf16[2,128,128]{2,1,0:T(8,128)(2,1)}, u32[]{:S(2)}) copy-start(bf16[2,128,128]{2,1,0:T(8,128)(2,1)} %param.20) | copy-start | bytes 196612
  131.9 67.4 %copy-start.4 = (bf16[2,128,128]{2,1,0:T(8,128)(2,1)S(1)}, bf16[2,128,128]{2,1,0:T(8,128)(2,1)}, u32[]{:S(2)}) copy-start(bf16[2,128,128]{2,1,0:T(8,128)(2,1)} %param.21) | copy-start | bytes 196612
  131.9 98.1 %reduce-scatter.9.cloned.1.call-start = ((), (), s32[]{:S(2)}) async-start(), calls=%async_computation.10 | async-start | bytes 589824 | tf_op jit(solution)/shard_map/reduce_scatter | solution.py:89
  143.4 132.0 %all-gather.3.cloned.1.call-start = ((), (), s32[]{:S(2)}) async-start(), calls=%async_computation.7 | async-start | bytes 1114112 | tf_op jit(solution)/shard_map/all_gather | solution.py:80
  200.9 149.3 %reduce-scatter.11.cloned.1.call-start = ((), (), s32[]{:S(2)}) async-start(), calls=%async_computation.11 | async-start | bytes 1114112 | tf_op jit(solution)/shard_map/reduce_scatter | solution.py:92
  248.7 135.7 %copy-start.1 = (bf16[64,128]{1,0:T(8,128)(2,1)S(1)}, bf16[64,128]{1,0:T(8,128)(2,1)}, u32[]{:S(2)}) copy-start(bf16[64,128]{1,0:T(8,128)(2,1)} %param.16) | copy-start | bytes 49156
  258.0 92.2 %copy-start.2 = (bf16[256,128]{1,0:T(8,128)(2,1)S(1)}, bf16[256,128]{1,0:T(8,128)(2,1)}, u32[]{:S(2)}) copy-start(bf16[256,128]{1,0:T(8,128)(2,1)} %fusion.13) | copy-start | bytes 196612
  258.0 123.7 %reduce-scatter.7.cloned.1.call-start = ((), (), s32[]{:S(2)}) async-start(), calls=%async_computation.8 | async-start | bytes 589824 | tf_op jit(solution)/shard_map/reduce_scatter | solution.py:89
Sparse Core Ops, SparseCore 0:
  77.1 37.4 all-gather.4
  132.0 66.1 reduce-scatter.4
  200.7 29.1 reduce-scatter.8
  232.5 42.7 all-gather.2
  278.4 71.7 reduce-scatter.10
  352.6 29.1 reduce-scatter.6
where the time goes:
time: 394 us; the launch traced here: 391 us
  waiting for transfers between devices  207 us (53%)
  matrix products  52.9 us (13%)
  other arithmetic  47.4 us (12%)
  blocking collectives  30.9 us (8%)
  local copies, waits for them, and re-layouts  19.8 us (5%)
  starting transfers between devices  18.9 us (5%)
  between operations  14.3 us (4%)
    reduce_scatter x2, waiting for transfers between devices, per_device(): lax.psum_scatter(item_part.astype(jnp.bfloat16), 'row', scatter_dimension...  118 us
    reduce_scatter x2, waiting for transfers between devices, per_device(): lax.psum_scatter(user_part.astype(jnp.bfloat16), 'col', scatter_dimension...  57.9 us
    all_gather x2, blocking collectives, per_device(): lax.all_gather(user_rows, 'col', axis=0, tiled=True)  30.9 us
    convert_element_type x1, other arithmetic, dequantize(): return tiled.reshape(row_count, columns).astype(jnp.bfloat16)  26.4 us
    dot_general x2, matrix products, per_device(): jnp.dot(adjacency, lax.all_gather(item_rows, 'row', axis=0, tiled=True),...  22.7 us
    dot_general x2, matrix products, per_device(): lax.dot_general(adjacency, lax.all_gather(user_rows, 'col', axis=0, tiled...  18.6 us
    scatter-add x1, other arithmetic, per_device(): jax.ops.segment_sum(chosen.reshape(-1, D), segment, num_segments=node_cou...  17.3 us
    all_gather x2, waiting for transfers between devices, per_device(): lax.all_gather(item_rows, 'row', axis=0, tiled=True)  17.3 us
  transfers between devices with their start and end apart: 8, of which 7 were waited for; matrix products, arithmetic and copies ran while one was open for 22% of the time, Pallas kernels for 0%

commit v1 on v0

v1 whole, which is shorter than its diff:
```python
import jax
import jax.numpy as jnp
from jax import lax
from jax.experimental import pallas as pl
from jax.experimental.pallas import tpu as pltpu
from jax.sharding import PartitionSpec as P

D = 128
RAW_COLS = 64
NARROW = 32
TILE = 128
LAYERS = 2
UPD = 256
IPD = 256
CAP = 24
ROWS = 16
COLS = 8
DEVICES = ROWS * COLS
RAW_DEV = 1024
USERS = UPD * COLS
ITEMS = IPD * ROWS
NODES = UPD + IPD
GROUP = 16
CHUNK = 768
SIDE = 4
HALF_D = D // 2
SCALED_FIRST = 10
USER_FIRST = 2

F32 = jnp.float32
BF16 = jnp.bfloat16
I32 = jnp.int32
MESH = pl.DeviceIdType.MESH


def dot(a, b):
    return jnp.dot(a, b, preferred_element_type=F32)


def dot_nt(a, b):
    return lax.dot_general(a, b, (((1,), (1,)), ((), ())), preferred_element_type=F32)


def wait_bytes(ref, sem):
    pltpu.make_async_copy(ref, ref, sem).wait()


def update(side, own, weight_sum, weight_product):
    own = own.astype(F32)
    linear = dot((side + own).astype(BF16), weight_sum)
    linear = linear + dot((side * own).astype(BF16), weight_product)
    return jnp.where(linear > 0, linear, 0.2 * linear).astype(BF16)


def kernel(
    raw_hbm,
    wide_hbm,
    dest_hbm,
    slot_hbm,
    narrow_hbm,
    proj_hbm,
    adj_hbm,
    mask_hbm,
    scale_hbm,
    weight_sum_hbm,
    weight_product_hbm,
    user_ref,
    item_ref,
    raw_ref,
    wide_ref,
    dest_ref,
    slot_ref,
    mask_ref,
    scale_ref,
    weight_sum_ref,
    weight_product_ref,
    adj,
    packed,
    place,
    send,
    by_row,
    by_col,
    recv,
    combined,
    totals,
    users,
    items,
    users_t,
    items_all,
    item_send,
    own_a,
    own_b,
    first_a,
    first_b,
    second_send,
    second_a,
    second_b,
    user_send,
    user_recv,
    user_own,
    in_sems,
    adj_sem,
    local_sem,
    row_sems,
    ut_sems,
    ia_sems,
    ir_sems,
    ur_sems,
):
    row = lax.axis_index("row")
    col = lax.axis_index("col")
    x = row // SIDE
    y = lax.rem(row, SIDE)
    row_odd = lax.rem(row, 2)
    col_odd = lax.rem(col, 2)
    odd = lax.rem(row + col, 2)

    inputs = [
        pltpu.make_async_copy(src, dst, in_sems.at[i])
        for i, (src, dst) in enumerate(
            (
                (dest_hbm, dest_ref),
                (slot_hbm, slot_ref),
                (wide_hbm, wide_ref),
                (raw_hbm, raw_ref),
                (mask_hbm, mask_ref),
                (scale_hbm, scale_ref),
                (proj_hbm, combined.at[0:RAW_COLS, :]),
                (narrow_hbm, combined.at[RAW_COLS : RAW_COLS + NARROW, :]),
                (weight_sum_hbm, weight_sum_ref),
                (weight_product_hbm, weight_product_ref),
            )
        )
    ]
    for copy in inputs[:4]:
        copy.start()

    barrier = pltpu.get_barrier_semaphore()

    def greet_row(k, carry):
        there = {"row": lax.rem(row + k, ROWS), "col": col}
        pl.semaphore_signal(barrier, inc=1, device_id=there, device_id_type=MESH)
        return carry

    def greet_col(k, carry):
        there = {"row": row, "col": lax.rem(col + k, COLS)}
        pl.semaphore_signal(barrier, inc=1, device_id=there, device_id_type=MESH)
        return carry

    lax.fori_loop(1, ROWS, greet_row, 0)
    lax.fori_loop(1, COLS, greet_col, 0)

    for copy in inputs[4:]:
        copy.start()

    def adj_copy(i):
        rows = pl.ds(pl.multiple_of(i * TILE, TILE), TILE)
        return pltpu.make_async_copy(adj_hbm.at[rows, :], adj.at[rows, :], adj_sem.at[i])

    def fetch(i, carry):
        adj_copy(i).start()
        return carry

    lax.fori_loop(0, USERS // TILE, fetch, 0)

    def push(src, dst, sems, there):
        pltpu.make_async_remote_copy(
            src_ref=src,
            dst_ref=dst,
            send_sem=sems.at[0],
            recv_sem=sems.at[1],
            device_id=there,
            device_id_type=MESH,
        ).start()

    for copy in inputs[:4]:
        copy.wait()
    dest = dest_ref[...]
    target = lax.broadcasted_iota(I32, (DEVICES, RAW_DEV), 0)
    hit = jnp.where(target == dest, 1.0, 0.0).astype(F32)
    earlier = jnp.where(
        lax.broadcasted_iota(I32, (256, 256), 0) < lax.broadcasted_iota(I32, (256, 256), 1), 1.0, 0.0
    ).astype(BF16)
    before = jnp.zeros((DEVICES, 1), F32)
    device = lax.broadcasted_iota(I32, (DEVICES, 256), 0)
    to_row, to_col = device // COLS, device % COLS
    space = jnp.where(
        (to_row + to_col) % 2 == 0,
        to_row * (COLS // 2) + to_col // 2,
        DEVICES // 2 + to_col * (ROWS // 2) + to_row // 2,
    )
    start = (space * CAP).astype(F32)
    for b in range(RAW_DEV // 256):
        part = hit[:, b * 256 : (b + 1) * 256]
        rank = dot(part.astype(BF16), earlier) + before
        place[0:1, b * 256 : (b + 1) * 256] = jnp.sum(
            part * (rank + start), axis=0, keepdims=True
        ).astype(I32)
        before = before + jnp.sum(part, axis=1, keepdims=True)

    slot = slot_ref[...]
    raw = raw_ref[...].astype(F32)
    wide_f = wide_ref[...].astype(F32)
    packed[0:RAW_COLS, :] = (raw * wide_f).astype(BF16)
    packed[RAW_COLS : RAW_COLS + NARROW, :] = (raw[0:NARROW] * (1.0 - wide_f)).astype(BF16)
    which = lax.broadcasted_iota(I32, (32, RAW_DEV), 0)
    codes = jnp.where(which == 0, slot // 2, jnp.where(which == 1, slot % 2, 0))
    packed[96:128, :] = codes.astype(F32).astype(BF16)

    def build(g):
        first = g * GROUP * CAP
        index = lax.broadcasted_iota(I32, (GROUP * CAP, RAW_DEV), 0) + first
        pick = jnp.where(index == place[0:1, :], 1.0, 0.0).astype(BF16)
        rows = dot_nt(pick, packed[...]).reshape(GROUP, CAP, D).astype(BF16)
        send[pl.ds(pl.multiple_of(g * GROUP, GROUP), GROUP)] = rows

    pl.semaphore_wait(barrier, ROWS + COLS - 2)

    half_row, half_col = COLS // 2, ROWS // 2

    def start_rows(i, carry):
        g = lax.rem(x + i, SIDE)
        build(g)

        def one(k, inner):
            other = g * SIDE + lax.rem(y + k, SIDE)
            src = send.at[pl.ds(pl.multiple_of(other * half_row, half_row), half_row)]

            @pl.when(other != row)
            def _():
                push(src, by_row.at[row], row_sems.at[0], {"row": other, "col": col})

            return inner

        return lax.fori_loop(0, SIDE, one, carry)

    lax.fori_loop(0, SIDE, start_rows, 0)

    def start_cols(i, carry):
        g = lax.rem(col // 2 + i, SIDE)
        build(g + SIDE)

        def one(k, inner):
            other = g * 2 + k
            first = DEVICES // 2 + other * half_col
            src = send.at[pl.ds(pl.multiple_of(first, half_col), half_col)]

            @pl.when(other != col)
            def _():
                push(src, by_col.at[col], row_sems.at[1], {"row": row, "col": other})

            return inner

        return lax.fori_loop(0, 2, one, carry)

    lax.fori_loop(0, SIDE, start_cols, 0)
    my_rows = send.at[pl.ds(pl.multiple_of(row * half_row, half_row), half_row)]
    my_cols = send.at[pl.ds(pl.multiple_of(DEVICES // 2 + col * half_col, half_col), half_col)]
    keep_rows = pltpu.make_async_copy(my_rows, by_row.at[row], local_sem.at[0])
    keep_cols = pltpu.make_async_copy(my_cols, by_col.at[col], local_sem.at[1])
    keep_rows.start()
    keep_cols.start()

    inputs[4].wait()
    inputs[5].wait()

    def scale_tiles(i, carry):
        adj_copy(i).wait()
        rows = pl.ds(pl.multiple_of(i * TILE, TILE), TILE)
        for j in range(ITEMS // TILE):
            factor = mask_ref[i, j].astype(F32) * scale_ref[i, j]
            columns = slice(j * TILE, (j + 1) * TILE)
            adj[rows, columns] = (adj[rows, columns].astype(F32) * factor).astype(BF16)
        return carry

    scaled_first = SCALED_FIRST
    lax.fori_loop(0, scaled_first, scale_tiles, 0)

    keep_rows.wait()
    keep_cols.wait()
    rest_rows = by_row.at[pl.ds(0, ROWS - 1)]
    rest_cols = by_col.at[pl.ds(0, COLS - 1)]
    wait_bytes(rest_rows, row_sems.at[0, 1])

    def along_col(j, carry):
        other = 2 * j + row_odd
        src = by_row.at[:, j]
        dst = recv.at[pl.ds(pl.multiple_of(col * ROWS, ROWS), ROWS)]

        @pl.when(other != col)
        def _():
            push(src, dst, row_sems.at[2], {"row": row, "col": other})

        @pl.when(other == col)
        def _():
            pltpu.make_async_copy(src, dst, local_sem.at[2]).start()

        return carry

    lax.fori_loop(0, half_row, along_col, 0)
    wait_bytes(rest_cols, row_sems.at[1, 1])

    def along_row(j, carry):
        other = 2 * j + 1 - col_odd
        src = by_col.at[:, j]
        dst = recv.at[pl.ds(pl.multiple_of(row * COLS, COLS), COLS)]

        @pl.when(other != row)
        def _():
            push(src, dst, row_sems.at[2], {"row": other, "col": col})

        @pl.when(other == row)
        def _():
            pltpu.make_async_copy(src, dst, local_sem.at[2]).start()

        return carry

    lax.fori_loop(0, half_col, along_row, 0)

    lax.fori_loop(scaled_first, USERS // TILE, scale_tiles, 0)
    combined[96:128, :] = jnp.zeros((32, D), BF16)
    totals[...] = jnp.zeros((NODES, D), F32)
    for copy in inputs[6:]:
        copy.wait()

    @pl.when(odd == 0)
    def _():
        wait_bytes(recv.at[pl.ds(0, ROWS)], local_sem.at[2])
        wait_bytes(recv.at[pl.ds(0, DEVICES - ROWS)], row_sems.at[2, 1])

    @pl.when(odd == 1)
    def _():
        wait_bytes(recv.at[pl.ds(0, COLS)], local_sem.at[2])
        wait_bytes(recv.at[pl.ds(0, DEVICES - COLS)], row_sems.at[2, 1])

    lane = lax.broadcasted_iota(I32, (8, D), 1)
    decode = jnp.where(lane == 96, 2.0, jnp.where(lane == 97, 1.0, 0.0)).astype(BF16)

    def add_chunk(i, carry):
        count = CHUNK // CAP
        rows = recv[pl.ds(pl.multiple_of(i * count, count), count)].reshape(CHUNK, D)
        slots = dot_nt(decode, rows)[0:1, :].astype(I32)
        pick = jnp.where(
            lax.broadcasted_iota(I32, (NODES, CHUNK), 0) == slots, 1.0, 0.0
        ).astype(BF16)
        totals[...] += dot(pick, rows)
        return carry

    lax.fori_loop(0, DEVICES * CAP // CHUNK, add_chunk, 0)
    total = totals[...]
    high = total.astype(BF16)
    left = total - high.astype(F32)
    middle = left.astype(BF16)
    low = (left - middle.astype(F32)).astype(BF16)
    projection = combined[...]
    initial = dot(high, projection) + (dot(middle, projection) + dot(low, projection))
    users[...] = initial[0:UPD].astype(BF16)
    items[...] = initial[UPD:NODES].astype(BF16)

    my_user_lanes = pl.ds(pl.multiple_of(col * UPD, UPD), UPD)

    def send_users(layer):
        users_t[layer, :, my_user_lanes] = jnp.transpose(users[...].astype(F32)).astype(BF16)
        block = users_t.at[layer, :, my_user_lanes]

        def one(k, carry):
            there = {"row": row, "col": lax.rem(col + k, COLS)}
            push(block, block, ut_sems.at[layer], there)
            return carry

        lax.fori_loop(1, COLS, one, 0)

    def ring_x(k):
        return lax.rem(x + k, SIDE) * SIDE + y

    def ring_y(k):
        return x * SIDE + lax.rem(y + k, SIDE)

    def half(layer, block, which):
        first = block * IPD + which * (IPD // 2)
        return items_all.at[layer, pl.ds(pl.multiple_of(first, IPD // 2), IPD // 2), :]

    def send_items(layer):
        items_all[layer, pl.ds(pl.multiple_of(row * IPD, IPD), IPD), :] = items[...]
        top, low_half = half(layer, row, 0), half(layer, row, 1)
        for step, (along, across) in enumerate(((ring_x, ring_y), (ring_y, ring_x))):
            for k in range(1, SIDE):
                push(top, top, ia_sems.at[layer, step], {"row": along(k), "col": col})
                push(low_half, low_half, ia_sems.at[layer, step], {"row": across(k), "col": col})

    def forward_items(layer):
        wait_bytes(items_all.at[layer, pl.ds(0, 3 * IPD), :], ia_sems.at[layer, 0, 1])
        for j in range(1, SIDE):
            top, low_half = half(layer, ring_x(j), 0), half(layer, ring_y(j), 1)
            for k in range(1, SIDE):
                push(top, top, ia_sems.at[layer, 1], {"row": ring_y(k), "col": col})
                push(low_half, low_half, ia_sems.at[layer, 1], {"row": ring_x(k), "col": col})

    def item_block(layer):
        def body(i, carry):
            to_x = lax.rem(x + 1 + i // 2, SIDE)
            first = to_x * SIDE + 2 * lax.rem(i, 2)
            lanes = pl.ds(pl.multiple_of(first * IPD, 2 * IPD), 2 * IPD)
            part = dot(users_t[layer], adj[:, lanes])
            for q in range(2):
                to = first + q
                to_y = lax.rem(to, SIDE)
                block = part[:, q * IPD : (q + 1) * IPD]
                item_send[to] = block.astype(BF16)

                @pl.when(to_y != y)
                def _():
                    ahead = lax.rem(to_y - y + SIDE, SIDE)
                    there = {"row": x * SIDE + to_y, "col": col}
                    push(
                        item_send.at[to, 0:HALF_D],
                        first_a.at[layer, ahead - 1, to_x],
                        ir_sems.at[layer, 0],
                        there,
                    )

                @pl.when(to_y == y)
                def _():
                    own_a[to_x] = block[0:HALF_D]

                @pl.when(to_x != x)
                def _():
                    ahead = lax.rem(to_x - x + SIDE, SIDE)
                    there = {"row": to_x * SIDE + y, "col": col}
                    push(
                        item_send.at[to, HALF_D:D],
                        first_b.at[layer, ahead - 1, to_y],
                        ir_sems.at[layer, 1],
                        there,
                    )

                @pl.when(to_x == x)
                def _():
                    own_b[to_y] = block[HALF_D:D]

            return carry

        lax.fori_loop(0, ROWS // 2, body, 0)

    def forward_sums(layer):
        wait_bytes(first_a.at[layer], ir_sems.at[layer, 0, 1])
        wait_bytes(first_b.at[layer], ir_sems.at[layer, 1, 1])
        for k in range(1, SIDE):
            to_x, to_y = lax.rem(x + k, SIDE), lax.rem(y + k, SIDE)
            for h, (own, came, to, there, land) in enumerate(
                (
                    (own_a, first_a, to_x, ring_x(k), second_a),
                    (own_b, first_b, to_y, ring_y(k), second_b),
                )
            ):
                total = own[to]
                for source in range(SIDE - 1):
                    total = total + came[layer, source, to].astype(F32)
                second_send[k - 1, h] = total.astype(BF16)
                push(
                    second_send.at[k - 1, h],
                    land.at[layer, k - 1],
                    ir_sems.at[layer, 2],
                    {"row": there, "col": col},
                )

    def item_side(layer):
        halves = []
        sums = ((own_a, first_a, x), (own_b, first_b, y))
        for own, came, here in sums:
            total = own[here]
            for source in range(SIDE - 1):
                total = total + came[layer, source, here].astype(F32)
            halves.append(total)
        wait_bytes(second_send, ir_sems.at[layer, 2, 1])
        for h, land in enumerate((second_a, second_b)):
            for source in range(SIDE - 1):
                halves[h] = halves[h] + land[layer, source].astype(F32)
        return jnp.transpose(jnp.concatenate(halves, axis=0))

    def user_block(layer):
        def body(i, carry):
            first = 2 * lax.rem(col // 2 + 1 + i, SIDE)
            rows = pl.ds(pl.multiple_of(first * UPD, 2 * UPD), 2 * UPD)
            part = dot(adj[rows, :], items_all[layer])
            for q in range(2):
                to = first + q
                block = part[q * UPD : (q + 1) * UPD]

                @pl.when(to != col)
                def _():
                    ahead = lax.rem(to - col + COLS, COLS)
                    user_send[ahead - 1] = block.astype(BF16)
                    push(
                        user_send.at[ahead - 1],
                        user_recv.at[layer, ahead - 1],
                        ur_sems.at[layer],
                        {"row": row, "col": to},
                    )

                @pl.when(to == col)
                def _():
                    user_own[...] = block

            return carry

        return body

    send_users(0)
    send_items(0)
    for layer in range(LAYERS):
        last = layer + 1 == LAYERS
        forward_items(layer)
        users_in = users_t.at[layer, :, pl.ds(0, (COLS - 1) * UPD)]
        wait_bytes(users_in, ut_sems.at[layer, 1])
        item_block(layer)
        second_in = items_all.at[layer, pl.ds(0, 12 * IPD), :]
        wait_bytes(second_in, ia_sems.at[layer, 1, 1])
        lax.fori_loop(0, USER_FIRST, user_block(layer), 0)
        forward_sums(layer)
        lax.fori_loop(USER_FIRST, SIDE, user_block(layer), 0)

        new_items = update(
            item_side(layer), items[...], weight_sum_ref[layer], weight_product_ref[layer]
        )
        if last:
            item_ref[...] = new_items
        else:
            items[...] = new_items
            send_items(layer + 1)

        wait_bytes(user_recv.at[layer], ur_sems.at[layer, 1])
        side = user_own[...]
        for k in range(COLS - 1):
            side = side + user_recv[layer, k].astype(F32)
        new_users = update(side, users[...], weight_sum_ref[layer], weight_product_ref[layer])
        if last:
            user_ref[...] = new_users
        else:
            users[...] = new_users
            send_users(layer + 1)

        wait_bytes(users_in, ut_sems.at[layer, 0])
        wait_bytes(items_all.at[layer, pl.ds(0, 3 * IPD), :], ia_sems.at[layer, 0, 0])
        wait_bytes(second_in, ia_sems.at[layer, 1, 0])
        wait_bytes(first_a.at[layer], ir_sems.at[layer, 0, 0])
        wait_bytes(first_b.at[layer], ir_sems.at[layer, 1, 0])
        wait_bytes(second_send, ir_sems.at[layer, 2, 0])
        wait_bytes(user_send, ur_sems.at[layer, 0])

    wait_bytes(rest_rows, row_sems.at[0, 0])
    wait_bytes(rest_cols, row_sems.at[1, 0])

    @pl.when(odd == 0)
    def _():
        wait_bytes(recv.at[pl.ds(0, DEVICES - ROWS)], row_sems.at[2, 0])

    @pl.when(odd == 1)
    def _():
        wait_bytes(recv.at[pl.ds(0, DEVICES - COLS)], row_sems.at[2, 0])


def per_device(
    raw_rows,
    raw_wide,
    raw_dest,
    raw_slot,
    proj_narrow,
    proj_wide,
    adj_values,
    tile_mask,
    tile_scale,
    weight_sum,
    weight_product,
):
    vmem = pl.BlockSpec(memory_space=pltpu.VMEM)
    hbm = pl.BlockSpec(memory_space=pltpu.HBM)
    dma = pltpu.SemaphoreType.DMA
    user_rows, item_rows = pl.pallas_call(
        kernel,
        out_shape=(
            jax.ShapeDtypeStruct((UPD, D), BF16),
            jax.ShapeDtypeStruct((IPD, D), BF16),
        ),
        in_specs=[hbm] * 11,
        out_specs=(vmem, vmem),
        scratch_shapes=[
            pltpu.VMEM((RAW_COLS, RAW_DEV), BF16),
            pltpu.VMEM((1, RAW_DEV), I32),
            pltpu.VMEM((1, RAW_DEV), I32),
            pltpu.VMEM((1, RAW_DEV), I32),
            pltpu.SMEM((USERS // TILE, ITEMS // TILE), I32),
            pltpu.SMEM((USERS // TILE, ITEMS // TILE), F32),
            pltpu.VMEM((LAYERS, D, D), BF16),
            pltpu.VMEM((LAYERS, D, D), BF16),
            pltpu.VMEM((USERS, ITEMS), BF16),
            pltpu.VMEM((D, RAW_DEV), BF16),
            pltpu.VMEM((8, RAW_DEV), I32),
            pltpu.VMEM((DEVICES, CAP, D), BF16),
            pltpu.VMEM((ROWS, COLS // 2, CAP, D), BF16),
            pltpu.VMEM((COLS, ROWS // 2, CAP, D), BF16),
            pltpu.VMEM((DEVICES, CAP, D), BF16),
            pltpu.VMEM((D, D), BF16),
            pltpu.VMEM((NODES, D), F32),
            pltpu.VMEM((UPD, D), BF16),
            pltpu.VMEM((IPD, D), BF16),
            pltpu.VMEM((LAYERS, D, USERS), BF16),
            pltpu.VMEM((LAYERS, ITEMS, D), BF16),
            pltpu.VMEM((ROWS, D, IPD), BF16),
            pltpu.VMEM((SIDE, HALF_D, IPD), F32),
            pltpu.VMEM((SIDE, HALF_D, IPD), F32),
            pltpu.VMEM((LAYERS, SIDE - 1, SIDE, HALF_D, IPD), BF16),
            pltpu.VMEM((LAYERS, SIDE - 1, SIDE, HALF_D, IPD), BF16),
            pltpu.VMEM((SIDE - 1, 2, HALF_D, IPD), BF16),
            pltpu.VMEM((LAYERS, SIDE - 1, HALF_D, IPD), BF16),
            pltpu.VMEM((LAYERS, SIDE - 1, HALF_D, IPD), BF16),
            pltpu.VMEM((COLS - 1, UPD, D), BF16),
            pltpu.VMEM((LAYERS, COLS - 1, UPD, D), BF16),
            pltpu.VMEM((UPD, D), F32),
            dma((10,)),
            dma((USERS // TILE,)),
            dma((3,)),
            dma((3, 2)),
            dma((LAYERS, 2)),
            dma((LAYERS, 2, 2)),
            dma((LAYERS, 3, 2)),
            dma((LAYERS, 2)),
        ],
        compiler_params=pltpu.CompilerParams(
            collective_id=0, has_side_effects=True, vmem_limit_bytes=56 << 20
        ),
    )(
        raw_rows.T,
        raw_wide.reshape(1, RAW_DEV),
        raw_dest.reshape(1, RAW_DEV),
        raw_slot.reshape(1, RAW_DEV),
        proj_narrow,
        proj_wide,
        adj_values,
        tile_mask,
        tile_scale,
        weight_sum,
        weight_product,
    )
    return (user_rows, item_rows[None])


def solution(mesh):
    placed = (
        P(("row", "col"), None),
        P(("row", "col")),
        P(("row", "col")),
        P(("row", "col")),
        P(),
        P(),
        P("row", "col"),
        P("row", "col"),
        P("row", "col"),
        P(),
        P(),
    )
    return jax.shard_map(
        per_device,
        mesh=mesh,
        in_specs=placed,
        out_specs=(P(("row", "col"), None), P("col", "row", None)),
        check_vma=False,
    )
```

time: 394 us -> 76.5 us (0.19)
  waiting for transfers between devices: 207 us -> 0 us
  Pallas kernels: 0 us -> 72.7 us
  matrix products: 52.9 us -> 0 us
  other arithmetic: 47.4 us -> 0 us
  blocking collectives: 30.9 us -> 0 us
  starting transfers between devices: 18.9 us -> 0 us
  local copies, waits for them, and re-layouts: 19.8 us -> 2.95 us
  between operations: 14.3 us -> 0.64 us
    reduce_scatter x4 -> x0, waiting for transfers between devices: 176 us -> none  [the longest x2 118 us: per_device(): lax.psum_scatter(item_part.astype(jnp.bfloat16), 'row', scatter_dimension...]
    pallas_call x0 -> x1, Pallas kernels: none -> 72.7 us  [per_device(): pl.pallas_call(kernel, out_shape=(jax.ShapeDtypeStruct((UPD, D), BF16), j...]
    dot_general x14 -> x0, matrix products: 52.9 us -> none  [the longest x2 22.7 us: per_device(): jnp.dot(adjacency, lax.all_gather(item_rows, 'row', axis=0, tiled=True),...]
    all_gather x2 -> x0, blocking collectives: 30.9 us -> none  [per_device(): lax.all_gather(user_rows, 'col', axis=0, tiled=True)]
    convert_element_type x1 -> x0, other arithmetic: 26.4 us -> none  [dequantize(): return tiled.reshape(row_count, columns).astype(jnp.bfloat16)]
    all_to_all x2 -> x0, starting transfers between devices: 18.4 us -> none  [the longest x1 11.5 us: per_device(): lax.all_to_all(send_codes, ('row', 'col'), split_axis=0, concat_axis=0, t...]
    scatter-add x1 -> x0, other arithmetic: 17.3 us -> none  [per_device(): jax.ops.segment_sum(chosen.reshape(-1, D), segment, num_segments=node_cou...]
    all_gather x2 -> x0, waiting for transfers between devices: 17.3 us -> none  [per_device(): lax.all_gather(item_rows, 'row', axis=0, tiled=True)]
  transfers between devices with their start and end apart: 8 -> 0, of which waited for: 7 -> 0; matrix products, arithmetic and copies ran while one was open for 22% -> 0% of each run, Pallas kernels for 0% -> 0%
where the time goes in v1:
time: 76.5 us; the launch traced here: 76.3 us
  Pallas kernels  72.7 us (95%)
  local copies, waits for them, and re-layouts  2.95 us (4%)
    pallas_call x1, Pallas kernels, per_device(): pl.pallas_call(kernel, out_shape=(jax.ShapeDtypeStruct((UPD, D), BF16), j...  72.7 us
    unnamed x2, local copies, waits for them, and re-layouts  2.95 us

profile of v1, /device:TPU:1, one launch (start us, length us, event | category | flops | bytes accessed | tf_op | source)
XLA Modules:
  0.0 76.3 jit_solution(5148014011567434061)
XLA Ops:
  0.6 72.7 %shard_map.122 = (bf16[256,128]{1,0:T(8,128)(2,1)}, bf16[256,128]{1,0:T(8,128)(2,1)}) custom-call(bf16[64,1024]{1,0:T(8,128)(2,1)} %bitcast.5, s32[1,1024]{1,0:T(1,128)} %bitcast.7, s32[1,1024]{1,0:T(1,128)} %bitcast.8, s32[1,1024]{1,0:T(1,128)} %bitcast.9, bf16[32,128]{1,0:T(8,128)(2,1)} %narrow_hbm.1, bf16[64,128]{1,0:T(8,128)(2,1)} %proj_hbm.1, ...), custom_call_target="tpu_custom_call" | custom-call | tf_op jit(solution)/shard_map/pallas_call | solution.py:579
  73.3 1.5 %copy.15 = bf16[256,128]{1,0:T(8,128)(2,1)} copy(bf16[256,128]{1,0:T(8,128)(2,1)} %get-tuple-element.8) | data formatting | bytes 131072
  74.8 1.5 %copy.16 = bf16[1,256,128]{2,1,0:T(8,128)(2,1)} copy(bf16[1,256,128]{2,1,0:T(8,128)(2,1)} %bitcast.6) | data formatting | bytes 131072

commit v2 on v1

--- a/solution.py
+++ b/solution.py
@@ -25,7 +25,6 @@
 SIDE = 4
 HALF_D = D // 2
 SCALED_FIRST = 10
-USER_FIRST = 2
 
 F32 = jnp.float32
 BF16 = jnp.bfloat16
@@ -101,16 +100,22 @@
     in_sems,
     adj_sem,
     local_sem,
-    row_sems,
-    ut_sems,
-    ia_sems,
-    ir_sems,
+    row_send,
+    row_recv,
+    chunk_sem,
+    ut_send,
+    ut_recv,
+    ia_send,
+    ia_recv,
+    ir_send,
+    ir_recv,
     ur_sems,
 ):
     row = lax.axis_index("row")
     col = lax.axis_index("col")
     x = row // SIDE
     y = lax.rem(row, SIDE)
+    z = col // 2
     row_odd = lax.rem(row, 2)
     col_odd = lax.rem(col, 2)
     odd = lax.rem(row + col, 2)
@@ -163,12 +168,12 @@
 
     lax.fori_loop(0, USERS // TILE, fetch, 0)
 
-    def push(src, dst, sems, there):
+    def push(src, dst, send_sem, recv_sem, there):
         pltpu.make_async_remote_copy(
             src_ref=src,
             dst_ref=dst,
-            send_sem=sems.at[0],
-            recv_sem=sems.at[1],
+            send_sem=send_sem,
+            recv_sem=recv_sem,
             device_id=there,
             device_id_type=MESH,
         ).start()
@@ -214,27 +219,23 @@
         rows = dot_nt(pick, packed[...]).reshape(GROUP, CAP, D).astype(BF16)
         send[pl.ds(pl.multiple_of(g * GROUP, GROUP), GROUP)] = rows
 
+    def build_rows(g, carry):
+        build(g)
+        return carry
+
+    lax.fori_loop(0, SIDE, build_rows, 0)
     pl.semaphore_wait(barrier, ROWS + COLS - 2)
 
     half_row, half_col = COLS // 2, ROWS // 2
 
-    def start_rows(i, carry):
-        g = lax.rem(x + i, SIDE)
-        build(g)
-
-        def one(k, inner):
-            other = g * SIDE + lax.rem(y + k, SIDE)
-            src = send.at[pl.ds(pl.multiple_of(other * half_row, half_row), half_row)]
-
-            @pl.when(other != row)
-            def _():
-                push(src, by_row.at[row], row_sems.at[0], {"row": other, "col": col})
-
-            return inner
-
-        return lax.fori_loop(0, SIDE, one, carry)
-
-    lax.fori_loop(0, SIDE, start_rows, 0)
+    def start_rows(k, carry):
+        other = lax.rem(row + k, ROWS)
+        src = send.at[pl.ds(pl.multiple_of(other * half_row, half_row), half_row)]
+        there = {"row": other, "col": col}
+        push(src, by_row.at[row], row_send.at[0], row_recv.at[0], there)
+        return carry
+
+    lax.fori_loop(1, ROWS, start_rows, 0)
 
     def start_cols(i, carry):
         g = lax.rem(col // 2 + i, SIDE)
@@ -247,7 +248,8 @@
 
             @pl.when(other != col)
             def _():
-                push(src, by_col.at[col], row_sems.at[1], {"row": row, "col": other})
+                there = {"row": row, "col": other}
+                push(src, by_col.at[col], row_send.at[1], row_recv.at[1], there)
 
             return inner
 
@@ -280,7 +282,7 @@
     keep_cols.wait()
     rest_rows = by_row.at[pl.ds(0, ROWS - 1)]
     rest_cols = by_col.at[pl.ds(0, COLS - 1)]
-    wait_bytes(rest_rows, row_sems.at[0, 1])
+    wait_bytes(rest_rows, row_recv.at[0])
 
     def along_col(j, carry):
         other = 2 * j + row_odd
@@ -289,7 +291,7 @@
 
         @pl.when(other != col)
         def _():
-            push(src, dst, row_sems.at[2], {"row": row, "col": other})
+            push(src, dst, row_send.at[2], chunk_sem.at[z], {"row": row, "col": other})
 
         @pl.when(other == col)
         def _():
@@ -298,7 +300,7 @@
         return carry
 
     lax.fori_loop(0, half_row, along_col, 0)
-    wait_bytes(rest_cols, row_sems.at[1, 1])
+    wait_bytes(rest_cols, row_recv.at[1])
 
     def along_row(j, carry):
         other = 2 * j + 1 - col_odd
@@ -307,7 +309,7 @@
 
         @pl.when(other != row)
         def _():
-            push(src, dst, row_sems.at[2], {"row": other, "col": col})
+            push(src, dst, row_send.at[2], chunk_sem.at[x], {"row": other, "col": col})
 
         @pl.when(other == row)
         def _():
@@ -319,34 +321,38 @@
 
     lax.fori_loop(scaled_first, USERS // TILE, scale_tiles, 0)
     combined[96:128, :] = jnp.zeros((32, D), BF16)
-    totals[...] = jnp.zeros((NODES, D), F32)
     for copy in inputs[6:]:
         copy.wait()
 
-    @pl.when(odd == 0)
-    def _():
-        wait_bytes(recv.at[pl.ds(0, ROWS)], local_sem.at[2])
-        wait_bytes(recv.at[pl.ds(0, DEVICES - ROWS)], row_sems.at[2, 1])
-
-    @pl.when(odd == 1)
-    def _():
-        wait_bytes(recv.at[pl.ds(0, COLS)], local_sem.at[2])
-        wait_bytes(recv.at[pl.ds(0, DEVICES - COLS)], row_sems.at[2, 1])
-
     lane = lax.broadcasted_iota(I32, (8, D), 1)
     decode = jnp.where(lane == 96, 2.0, jnp.where(lane == 97, 1.0, 0.0)).astype(BF16)
 
-    def add_chunk(i, carry):
+    def add_chunk(i):
         count = CHUNK // CAP
         rows = recv[pl.ds(pl.multiple_of(i * count, count), count)].reshape(CHUNK, D)
         slots = dot_nt(decode, rows)[0:1, :].astype(I32)
         pick = jnp.where(
             lax.broadcasted_iota(I32, (NODES, CHUNK), 0) == slots, 1.0, 0.0
         ).astype(BF16)
-        totals[...] += dot(pick, rows)
-        return carry
-
-    lax.fori_loop(0, DEVICES * CAP // CHUNK, add_chunk, 0)
+        return dot(pick, rows)
+
+    nearest = odd * x + (1 - odd) * z
+
+    @pl.when(odd == 0)
+    def _():
+        wait_bytes(recv.at[pl.ds(0, ROWS)], local_sem.at[2])
+        wait_bytes(recv.at[pl.ds(0, ROWS)], chunk_sem.at[nearest])
+
+    @pl.when(odd == 1)
+    def _():
+        wait_bytes(recv.at[pl.ds(0, COLS)], local_sem.at[2])
+        wait_bytes(recv.at[pl.ds(0, 3 * COLS)], chunk_sem.at[nearest])
+
+    totals[...] = add_chunk(nearest)
+    for step in (1, 3, 2):
+        chunk = lax.rem(nearest + step, SIDE)
+        wait_bytes(recv.at[pl.ds(0, DEVICES // SIDE)], chunk_sem.at[chunk])
+        totals[...] += add_chunk(chunk)
     total = totals[...]
     high = total.astype(BF16)
     left = total - high.astype(F32)
@@ -359,16 +365,24 @@
 
     my_user_lanes = pl.ds(pl.multiple_of(col * UPD, UPD), UPD)
 
+    def user_lanes(layer, owner):
+        lanes = pl.ds(pl.multiple_of(owner * UPD, UPD), UPD)
+        return users_t.at[layer, :, lanes]
+
+    partner = {"row": row, "col": col + 1 - 2 * col_odd}
+
     def send_users(layer):
         users_t[layer, :, my_user_lanes] = jnp.transpose(users[...].astype(F32)).astype(BF16)
-        block = users_t.at[layer, :, my_user_lanes]
-
-        def one(k, carry):
-            there = {"row": row, "col": lax.rem(col + k, COLS)}
-            push(block, block, ut_sems.at[layer], there)
-            return carry
-
-        lax.fori_loop(1, COLS, one, 0)
+        block = user_lanes(layer, col)
+        for k in (1, 3, 2):
+            there = {"row": row, "col": lax.rem(col + 2 * k, COLS)}
+            push(block, block, ut_send.at[layer, 0], ut_recv.at[layer, k], there)
+        push(block, block, ut_send.at[layer, 1], ut_recv.at[layer, 0], partner)
+
+    def forward_users(layer, k):
+        block = user_lanes(layer, lax.rem(col + COLS - 2 * k, COLS))
+        wait_bytes(block, ut_recv.at[layer, k])
+        push(block, block, ut_send.at[layer, 1], ut_recv.at[layer, 0], partner)
 
     def ring_x(k):
         return lax.rem(x + k, SIDE) * SIDE + y
@@ -382,19 +396,26 @@
 
     def send_items(layer):
         items_all[layer, pl.ds(pl.multiple_of(row * IPD, IPD), IPD), :] = items[...]
-        top, low_half = half(layer, row, 0), half(layer, row, 1)
-        for step, (along, across) in enumerate(((ring_x, ring_y), (ring_y, ring_x))):
-            for k in range(1, SIDE):
-                push(top, top, ia_sems.at[layer, step], {"row": along(k), "col": col})
-                push(low_half, low_half, ia_sems.at[layer, step], {"row": across(k), "col": col})
-
-    def forward_items(layer):
-        wait_bytes(items_all.at[layer, pl.ds(0, 3 * IPD), :], ia_sems.at[layer, 0, 1])
-        for j in range(1, SIDE):
-            top, low_half = half(layer, ring_x(j), 0), half(layer, ring_y(j), 1)
-            for k in range(1, SIDE):
-                push(top, top, ia_sems.at[layer, 1], {"row": ring_y(k), "col": col})
-                push(low_half, low_half, ia_sems.at[layer, 1], {"row": ring_x(k), "col": col})
+        top, bottom = half(layer, row, 0), half(layer, row, 1)
+        for k in (1, 3, 2):
+            along, across = {"row": ring_x(k), "col": col}, {"row": ring_y(k), "col": col}
+            push(top, top, ia_send.at[layer, 0], ia_recv.at[layer, 0, k], along)
+            push(bottom, bottom, ia_send.at[layer, 0], ia_recv.at[layer, 1, k], across)
+        for k in (1, 3, 2):
+            along, across = {"row": ring_x(k), "col": col}, {"row": ring_y(k), "col": col}
+            push(top, top, ia_send.at[layer, 1], ia_recv.at[layer, 0, 0], across)
+            push(bottom, bottom, ia_send.at[layer, 1], ia_recv.at[layer, 1, 0], along)
+
+    def forward_items(layer, j):
+        top, bottom = half(layer, ring_x(SIDE - j), 0), half(layer, ring_y(SIDE - j), 1)
+        wait_bytes(top, ia_recv.at[layer, 0, j])
+        for k in (1, 3, 2):
+            across = {"row": ring_y(k), "col": col}
+            push(top, top, ia_send.at[layer, 1], ia_recv.at[layer, 0, 0], across)
+        wait_bytes(bottom, ia_recv.at[layer, 1, j])
+        for k in (1, 3, 2):
+            along = {"row": ring_x(k), "col": col}
+            push(bottom, bottom, ia_send.at[layer, 1], ia_recv.at[layer, 1, 0], along)
 
     def item_block(layer):
         def body(i, carry):
@@ -415,7 +436,8 @@
                     push(
                         item_send.at[to, 0:HALF_D],
                         first_a.at[layer, ahead - 1, to_x],
-                        ir_sems.at[layer, 0],
+                        ir_send.at[layer, 0],
+                        ir_recv.at[layer, 0, to_x],
                         there,
                     )
 
@@ -430,7 +452,8 @@
                     push(
                         item_send.at[to, HALF_D:D],
                         first_b.at[layer, ahead - 1, to_y],
-                        ir_sems.at[layer, 1],
+                        ir_send.at[layer, 0],
+                        ir_recv.at[layer, 1, to_y],
                         there,
                     )
 
@@ -442,37 +465,28 @@
 
         lax.fori_loop(0, ROWS // 2, body, 0)
 
-    def forward_sums(layer):
-        wait_bytes(first_a.at[layer], ir_sems.at[layer, 0, 1])
-        wait_bytes(first_b.at[layer], ir_sems.at[layer, 1, 1])
-        for k in range(1, SIDE):
-            to_x, to_y = lax.rem(x + k, SIDE), lax.rem(y + k, SIDE)
-            for h, (own, came, to, there, land) in enumerate(
-                (
-                    (own_a, first_a, to_x, ring_x(k), second_a),
-                    (own_b, first_b, to_y, ring_y(k), second_b),
-                )
-            ):
-                total = own[to]
-                for source in range(SIDE - 1):
-                    total = total + came[layer, source, to].astype(F32)
-                second_send[k - 1, h] = total.astype(BF16)
-                push(
-                    second_send.at[k - 1, h],
-                    land.at[layer, k - 1],
-                    ir_sems.at[layer, 2],
-                    {"row": there, "col": col},
-                )
+    def first_sum(layer, h, to):
+        own, came = ((own_a, first_a), (own_b, first_b))[h]
+        wait_bytes(second_send.at[:, 0], ir_recv.at[layer, h, to])
+        total = own[to]
+        for source in range(SIDE - 1):
+            total = total + came[layer, source, to].astype(F32)
+        return total
+
+    def forward_sum(layer, h, k):
+        to = lax.rem((x, y)[h] + k, SIDE)
+        second_send[k - 1, h] = first_sum(layer, h, to).astype(BF16)
+        push(
+            second_send.at[k - 1, h],
+            (second_a, second_b)[h].at[layer, k - 1],
+            ir_send.at[layer, 1],
+            ir_recv.at[layer, 2, 0],
+            {"row": (ring_x, ring_y)[h](k), "col": col},
+        )
 
     def item_side(layer):
-        halves = []
-        sums = ((own_a, first_a, x), (own_b, first_b, y))
-        for own, came, here in sums:
-            total = own[here]
-            for source in range(SIDE - 1):
-                total = total + came[layer, source, here].astype(F32)
-            halves.append(total)
-        wait_bytes(second_send, ir_sems.at[layer, 2, 1])
+        halves = [first_sum(layer, 0, x), first_sum(layer, 1, y)]
+        wait_bytes(second_send, ir_recv.at[layer, 2, 0])
         for h, land in enumerate((second_a, second_b)):
             for source in range(SIDE - 1):
                 halves[h] = halves[h] + land[layer, source].astype(F32)
@@ -494,7 +508,8 @@
                     push(
                         user_send.at[ahead - 1],
                         user_recv.at[layer, ahead - 1],
-                        ur_sems.at[layer],
+                        ur_sems.at[layer, 0],
+                        ur_sems.at[layer, 1],
                         {"row": row, "col": to},
                     )
 
@@ -510,15 +525,24 @@
     send_items(0)
     for layer in range(LAYERS):
         last = layer + 1 == LAYERS
-        forward_items(layer)
-        users_in = users_t.at[layer, :, pl.ds(0, (COLS - 1) * UPD)]
-        wait_bytes(users_in, ut_sems.at[layer, 1])
+        for k in (1, 3, 2):
+            forward_items(layer, k)
+        for k in (1, 3, 2):
+            forward_users(layer, k)
+        wait_bytes(users_t.at[layer, :, pl.ds(0, 4 * UPD)], ut_recv.at[layer, 0])
         item_block(layer)
-        second_in = items_all.at[layer, pl.ds(0, 12 * IPD), :]
-        wait_bytes(second_in, ia_sems.at[layer, 1, 1])
-        lax.fori_loop(0, USER_FIRST, user_block(layer), 0)
-        forward_sums(layer)
-        lax.fori_loop(USER_FIRST, SIDE, user_block(layer), 0)
+        gathered = items_all.at[layer, pl.ds(0, 6 * IPD), :]
+        wait_bytes(gathered, ia_recv.at[layer, 0, 0])
+        wait_bytes(gathered, ia_recv.at[layer, 1, 0])
+        blocks = user_block(layer)
+        lax.fori_loop(0, 3, blocks, 0)
+        forward_sum(layer, 0, 1)
+        forward_sum(layer, 0, 2)
+        forward_sum(layer, 0, 3)
+        forward_sum(layer, 1, 1)
+        forward_sum(layer, 1, 2)
+        forward_sum(layer, 1, 3)
+        lax.fori_loop(3, 4, blocks, 0)
 
         new_items = update(
             item_side(layer), items[...], weight_sum_ref[layer], weight_product_ref[layer]
@@ -540,24 +564,25 @@
             users[...] = new_users
             send_users(layer + 1)
 
-        wait_bytes(users_in, ut_sems.at[layer, 0])
-        wait_bytes(items_all.at[layer, pl.ds(0, 3 * IPD), :], ia_sems.at[layer, 0, 0])
-        wait_bytes(second_in, ia_sems.at[layer, 1, 0])
-        wait_bytes(first_a.at[layer], ir_sems.at[layer, 0, 0])
-        wait_bytes(first_b.at[layer], ir_sems.at[layer, 1, 0])
-        wait_bytes(second_send, ir_sems.at[layer, 2, 0])
+        wait_bytes(users_t.at[layer, :, pl.ds(0, 3 * UPD)], ut_send.at[layer, 0])
+        wait_bytes(users_t.at[layer, :, pl.ds(0, 4 * UPD)], ut_send.at[layer, 1])
+        wait_bytes(items_all.at[layer, pl.ds(0, 3 * IPD), :], ia_send.at[layer, 0])
+        wait_bytes(items_all.at[layer, pl.ds(0, 12 * IPD), :], ia_send.at[layer, 1])
+        wait_bytes(first_a.at[layer], ir_send.at[layer, 0])
+        wait_bytes(first_b.at[layer], ir_send.at[layer, 0])
+        wait_bytes(second_send, ir_send.at[layer, 1])
         wait_bytes(user_send, ur_sems.at[layer, 0])
 
-    wait_bytes(rest_rows, row_sems.at[0, 0])
-    wait_bytes(rest_cols, row_sems.at[1, 0])
+    wait_bytes(rest_rows, row_send.at[0])
+    wait_bytes(rest_cols, row_send.at[1])
 
     @pl.when(odd == 0)
     def _():
-        wait_bytes(recv.at[pl.ds(0, DEVICES - ROWS)], row_sems.at[2, 0])
+        wait_bytes(recv.at[pl.ds(0, DEVICES - ROWS)], row_send.at[2])
 
     @pl.when(odd == 1)
     def _():
-        wait_bytes(recv.at[pl.ds(0, DEVICES - COLS)], row_sems.at[2, 0])
+        wait_bytes(recv.at[pl.ds(0, DEVICES - COLS)], row_send.at[2])
 
 
 def per_device(
@@ -578,10 +603,7 @@
     dma = pltpu.SemaphoreType.DMA
     user_rows, item_rows = pl.pallas_call(
         kernel,
-        out_shape=(
-            jax.ShapeDtypeStruct((UPD, D), BF16),
-            jax.ShapeDtypeStruct((IPD, D), BF16),
-        ),
+        out_shape=(pltpu.VMEM((UPD, D), BF16), pltpu.VMEM((IPD, D), BF16)),
         in_specs=[hbm] * 11,
         out_specs=(vmem, vmem),
         scratch_shapes=[
@@ -620,10 +642,15 @@
             dma((10,)),
             dma((USERS // TILE,)),
             dma((3,)),
-            dma((3, 2)),
+            dma((3,)),
+            dma((2,)),
+            dma((SIDE,)),
             dma((LAYERS, 2)),
-            dma((LAYERS, 2, 2)),
-            dma((LAYERS, 3, 2)),
+            dma((LAYERS, SIDE)),
+            dma((LAYERS, 2)),
+            dma((LAYERS, 2, SIDE)),
+            dma((LAYERS, 2)),
+            dma((LAYERS, 3, SIDE)),
             dma((LAYERS, 2)),
         ],
         compiler_params=pltpu.CompilerParams(

time: 76.5 us -> 69.9 us (0.914)
  Pallas kernels: 72.7 us -> 67.9 us
  local copies, waits for them, and re-layouts: 2.95 us -> 1.26 us
    pallas_call x1, Pallas kernels: 72.7 us -> 67.9 us  [per_device(): pl.pallas_call(kernel, out_shape=(pltpu.VMEM((UPD, D), BF16), pltpu.VMEM(...]
    unnamed x2, local copies, waits for them, and re-layouts: 2.95 us -> 1.26 us
where the time goes in v2:
time: 69.9 us; the launch traced here: 69.8 us
  Pallas kernels  67.9 us (97%)
  local copies, waits for them, and re-layouts  1.26 us (2%)
    pallas_call x1, Pallas kernels, per_device(): pl.pallas_call(kernel, out_shape=(pltpu.VMEM((UPD, D), BF16), pltpu.VMEM(...  67.9 us

profile of v2, /device:TPU:1, one launch (start us, length us, event | category | flops | bytes accessed | tf_op | source)
XLA Modules:
  0.0 69.8 jit_solution(16796495192580630494)
XLA Ops:
  0.6 67.9 %shard_map.122 = (bf16[256,128]{1,0:T(8,128)(2,1)S(1)}, bf16[256,128]{1,0:T(8,128)(2,1)S(1)}) custom-call(bf16[64,1024]{1,0:T(8,128)(2,1)} %bitcast.6, s32[1,1024]{1,0:T(1,128)} %bitcast.7, s32[1,1024]{1,0:T(1,128)} %bitcast.8, s32[1,1024]{1,0:T(1,128)} %bitcast.9, bf16[32,128]{1,0:T(8,128)(2,1)} %narrow_hbm.1, bf16[64,128]{1,0:T(8,128)(2,1)} %proj_hbm.1, ...), custom_call_target="tpu_custom_call" | custom-call | tf_op jit(solution)/shard_map/pallas_call | solution.py:604
  68.5 0.6 copy.15
  69.2 0.6 copy.16

commit v3 on v2

--- a/solution.py
+++ b/solution.py
@@ -24,7 +24,7 @@
 CHUNK = 768
 SIDE = 4
 HALF_D = D // 2
-SCALED_FIRST = 10
+SCALED_STEP = 2
 
 F32 = jnp.float32
 BF16 = jnp.bfloat16
@@ -232,7 +232,7 @@
         other = lax.rem(row + k, ROWS)
         src = send.at[pl.ds(pl.multiple_of(other * half_row, half_row), half_row)]
         there = {"row": other, "col": col}
-        push(src, by_row.at[row], row_send.at[0], row_recv.at[0], there)
+        push(src, by_row.at[row], row_send.at[0], row_recv.at[0, x], there)
         return carry
 
     lax.fori_loop(1, ROWS, start_rows, 0)
@@ -249,7 +249,7 @@
             @pl.when(other != col)
             def _():
                 there = {"row": row, "col": other}
-                push(src, by_col.at[col], row_send.at[1], row_recv.at[1], there)
+                push(src, by_col.at[col], row_send.at[1], row_recv.at[1, z], there)
 
             return inner
 
@@ -275,51 +275,64 @@
             adj[rows, columns] = (adj[rows, columns].astype(F32) * factor).astype(BF16)
         return carry
 
-    scaled_first = SCALED_FIRST
-    lax.fori_loop(0, scaled_first, scale_tiles, 0)
-
-    keep_rows.wait()
-    keep_cols.wait()
     rest_rows = by_row.at[pl.ds(0, ROWS - 1)]
     rest_cols = by_col.at[pl.ds(0, COLS - 1)]
-    wait_bytes(rest_rows, row_recv.at[0])
-
-    def along_col(j, carry):
-        other = 2 * j + row_odd
-        src = by_row.at[:, j]
-        dst = recv.at[pl.ds(pl.multiple_of(col * ROWS, ROWS), ROWS)]
-
-        @pl.when(other != col)
-        def _():
-            push(src, dst, row_send.at[2], chunk_sem.at[z], {"row": row, "col": other})
-
-        @pl.when(other == col)
-        def _():
-            pltpu.make_async_copy(src, dst, local_sem.at[2]).start()
-
-        return carry
-
-    lax.fori_loop(0, half_row, along_col, 0)
-    wait_bytes(rest_cols, row_recv.at[1])
-
-    def along_row(j, carry):
-        other = 2 * j + 1 - col_odd
-        src = by_col.at[:, j]
-        dst = recv.at[pl.ds(pl.multiple_of(row * COLS, COLS), COLS)]
-
-        @pl.when(other != row)
-        def _():
-            push(src, dst, row_send.at[2], chunk_sem.at[x], {"row": other, "col": col})
-
-        @pl.when(other == row)
-        def _():
-            pltpu.make_async_copy(src, dst, local_sem.at[2]).start()
-
-        return carry
-
-    lax.fori_loop(0, half_col, along_row, 0)
-
-    lax.fori_loop(scaled_first, USERS // TILE, scale_tiles, 0)
+
+    def along_col(g):
+        sources = pl.ds(pl.multiple_of(g * SIDE, SIDE), SIDE)
+        landing = recv.at[pl.ds(pl.multiple_of(col * ROWS + g * SIDE, SIDE), SIDE)]
+
+        def one(j, carry):
+            other = 2 * j + row_odd
+            src = by_row.at[sources, j]
+
+            @pl.when(other != col)
+            def _():
+                push(src, landing, row_send.at[2], chunk_sem.at[z], {"row": row, "col": other})
+
+            @pl.when(other == col)
+            def _():
+                pltpu.make_async_copy(src, landing, local_sem.at[2]).start()
+
+            return carry
+
+        lax.fori_loop(0, half_row, one, 0)
+
+    def along_row(g):
+        sources = pl.ds(pl.multiple_of(g * 2, 2), 2)
+        landing = recv.at[pl.ds(pl.multiple_of(row * COLS + g * 2, 2), 2)]
+
+        def one(j, carry):
+            other = 2 * j + 1 - col_odd
+            src = by_col.at[sources, j]
+
+            @pl.when(other != row)
+            def _():
+                push(src, landing, row_send.at[2], chunk_sem.at[x], {"row": other, "col": col})
+
+            @pl.when(other == row)
+            def _():
+                pltpu.make_async_copy(src, landing, local_sem.at[2]).start()
+
+            return carry
+
+        lax.fori_loop(0, half_col, one, 0)
+
+    scaled = 0
+    for step in (0, 1, 3, 2):
+        lax.fori_loop(scaled, scaled + SCALED_STEP, scale_tiles, 0)
+        scaled += SCALED_STEP
+        from_x, from_z = lax.rem(x + step, SIDE), lax.rem(z + step, SIDE)
+        if step == 0:
+            keep_rows.wait()
+            keep_cols.wait()
+        near = 1 if step == 0 else 0
+        wait_bytes(by_col.at[pl.ds(0, 2 - near)], row_recv.at[1, from_z])
+        along_row(from_z)
+        wait_bytes(by_row.at[pl.ds(0, SIDE - near)], row_recv.at[0, from_x])
+        along_col(from_x)
+
+    lax.fori_loop(scaled, USERS // TILE, scale_tiles, 0)
     combined[96:128, :] = jnp.zeros((32, D), BF16)
     for copy in inputs[6:]:
         copy.wait()
@@ -643,7 +656,7 @@
             dma((USERS // TILE,)),
             dma((3,)),
             dma((3,)),
-            dma((2,)),
+            dma((2, SIDE)),
             dma((SIDE,)),
             dma((LAYERS, 2)),
             dma((LAYERS, SIDE)),

time: 69.9 us -> 68.7 us (0.983)
  Pallas kernels: 67.9 us -> 66.6 us
    pallas_call x1, Pallas kernels: 67.9 us -> 66.6 us  [per_device(): pl.pallas_call(kernel, out_shape=(pltpu.VMEM((UPD, D), BF16), pltpu.VMEM(...]
where the time goes in v3:
time: 68.7 us; the launch traced here: 68.5 us
  Pallas kernels  66.6 us (97%)
  local copies, waits for them, and re-layouts  1.26 us (2%)
    pallas_call x1, Pallas kernels, per_device(): pl.pallas_call(kernel, out_shape=(pltpu.VMEM((UPD, D), BF16), pltpu.VMEM(...  66.6 us

profile of v3, /device:TPU:1, one launch (start us, length us, event | category | flops | bytes accessed | tf_op | source)
XLA Modules:
  0.0 68.5 jit_solution(16308494400555434815)
XLA Ops:
  0.6 66.6 %shard_map.122 = (bf16[256,128]{1,0:T(8,128)(2,1)S(1)}, bf16[256,128]{1,0:T(8,128)(2,1)S(1)}) custom-call(bf16[64,1024]{1,0:T(8,128)(2,1)} %bitcast.6, s32[1,1024]{1,0:T(1,128)} %bitcast.7, s32[1,1024]{1,0:T(1,128)} %bitcast.8, s32[1,1024]{1,0:T(1,128)} %bitcast.9, bf16[32,128]{1,0:T(8,128)(2,1)} %narrow_hbm.1, bf16[64,128]{1,0:T(8,128)(2,1)} %proj_hbm.1, ...), custom_call_target="tpu_custom_call" | custom-call | tf_op jit(solution)/shard_map/pallas_call | solution.py:617
  67.3 0.6 copy.15
  67.9 0.6 copy.16
